TPU v7x, 32 devices: a whole 2x2x4 slice. The times are simulated.
32 devices in a mesh: path: 4 (over z), trade: 8 (over y, x, core).
Axes of the slice: x: 2, y: 2, z: 4, core: 2. Of those that a mesh axis runs over, the one named last changes fastest.
Arguments:
- factors: bfloat16 [32, 8, 512], P(None, None, 'path'), may hold values from -5 to 5
- loadings: bfloat16 [32, 8, 32768], P(None, None, 'trade'), may hold values from -0.5 to 0.5
- notional: float32 [32768], P('trade'), may hold values from -1 to 1
- strike: float32 [32768], P('trade'), may hold values from 0.5 to 1.5
- date_weight: float32 [32], replicated, may hold values from 0.3 to 3
- loss_spanning: float32 [128], replicated, may hold values from 0.2 to 0.9
- loss_local: float32 [1024], P('trade'), may hold values from 0.2 to 0.9
- trade_slot: int32 [32768], P('trade'), may hold values from 0 to 255
- span_list: int32 [1024], P('trade'), may hold values from 0 to 127, as said below
Outputs:
- loading_grad: float32 [32, 8, 32768], P('path', None, 'trade')
- factor_grad: float32 [32, 8, 512], P('trade', None, 'path')
Inputs may be any that keep to these rules, and one draw needn't show every extreme that they name: `trade_slot`: slot s < 128 of a trade shard holds that shard's spanning set from span_list; slot 128 + i holds the shard's i-th local set. `span_list`: the 128 entries of one trade shard are distinct spanning set ids.
All inputs are finite; a program needn't handle non-finite values.
Results may differ from a plain program's by a relative error of at most 0.0021.
Values may be sent and summed in bfloat16 or wider, within the bound.
A program may use at most 64 MiB of HBM per device.

v0:
```python
import math
import jax
import jax.numpy as jnp
from jax import lax
from jax.sharding import PartitionSpec as P

smoothing = 0.5


def price(factor_block, loading_block):
    exponent = jnp.einsum(
        "bfp,bfk->bpk", factor_block, loading_block, preferred_element_type=jnp.float32
    )
    return jnp.exp(exponent)


def on_device(
    factors,
    loadings,
    notional,
    strike,
    date_weight,
    loss_spanning,
    loss_local,
    trade_slot,
    span_list,
):
    path_total = lax.axis_size("path") * factors.shape[2]
    factor_here = lax.all_to_all(factors, "path", split_axis=0, concat_axis=2, tiled=True)
    dates_here = factor_here.shape[0]
    first_date = lax.axis_index("path") * dates_here
    loading_here = lax.dynamic_slice_in_dim(loadings, first_date, dates_here, 0)
    weight_here = lax.dynamic_slice_in_dim(date_weight, first_date, dates_here, 0)
    date_count = factor_here.shape[0]
    factor_count = factor_here.shape[1]
    path_local = factor_here.shape[2]
    trade_local = loading_here.shape[2]
    span_local = span_list.shape[0]
    span_count = loss_spanning.shape[0]
    slot_count = span_local + loss_local.shape[0]
    dates_per_step = math.gcd(date_count, max(1, 512 // path_local))
    block_count = date_count // dates_per_step
    slot_table = (trade_slot[:, None] == jnp.arange(slot_count, dtype=jnp.int32)[None, :]).astype(
        jnp.bfloat16
    )
    set_match = span_list[:, None] == jnp.arange(span_count, dtype=jnp.int32)[None, :]
    set_table = set_match.astype(jnp.float32)
    set_select = set_match.astype(jnp.bfloat16)
    factor_blocks = factor_here.reshape(block_count, dates_per_step, factor_count, path_local)
    loading_blocks = loading_here.reshape(block_count, dates_per_step, factor_count, trade_local)
    weight_blocks = weight_here.reshape(block_count, dates_per_step)

    def forward(operands):
        factor_block, loading_block, weight_block = operands
        growth = price(factor_block, loading_block)
        values = (notional * (growth - strike)).astype(jnp.bfloat16)
        partial_sums = jnp.einsum(
            "bpk,ks->bps", values, slot_table, preferred_element_type=jnp.float32
        )
        span_part = jnp.einsum(
            "bps,sn->bpn",
            partial_sums[:, :, :span_local],
            set_table,
            precision=lax.Precision.HIGHEST,
            preferred_element_type=jnp.float32,
        )
        local_weight = (
            weight_block[:, None, None]
            * loss_local
            * jax.nn.sigmoid(partial_sums[:, :, span_local:] / smoothing)
        ).astype(jnp.bfloat16)
        return (span_part, local_weight)

    span_parts, local_weights = lax.map(forward, (factor_blocks, loading_blocks, weight_blocks))
    span_parts = span_parts.reshape(date_count, path_local, span_count)
    span_total = lax.psum(span_parts, "trade")
    span_weight = (
        weight_here[:, None, None] * loss_spanning * jax.nn.sigmoid(span_total / smoothing)
    ).astype(jnp.bfloat16)
    span_blocks = span_weight.reshape(block_count, dates_per_step, path_local, span_count)

    def adjoint(operands):
        factor_block, loading_block, span_block, local_block = operands
        growth = price(factor_block, loading_block)
        span_slots = jnp.einsum(
            "bpn,sn->bps", span_block, set_select, preferred_element_type=jnp.float32
        ).astype(jnp.bfloat16)
        slot_weight = jnp.concatenate([span_slots, local_block], axis=2)
        trade_weight = jnp.einsum(
            "bps,ks->bpk", slot_weight, slot_table, preferred_element_type=jnp.float32
        )
        sensitivity = (trade_weight * notional * growth).astype(jnp.bfloat16)
        loading_term = jnp.einsum(
            "bfp,bpk->bfk", factor_block, sensitivity, preferred_element_type=jnp.float32
        )
        factor_term = jnp.einsum(
            "bfk,bpk->bfp", loading_block, sensitivity, preferred_element_type=jnp.float32
        )
        return (loading_term, factor_term)

    loading_terms, factor_terms = lax.map(
        adjoint, (factor_blocks, loading_blocks, span_blocks, local_weights)
    )
    loading_terms = loading_terms.reshape(date_count, factor_count, trade_local)
    factor_terms = factor_terms.reshape(date_count, factor_count, path_local)
    loading_grad = loading_terms / path_total
    regrouped = lax.all_to_all(factor_terms, "path", split_axis=2, concat_axis=0, tiled=True)
    factor_grad = lax.psum_scatter(regrouped, "trade", scatter_dimension=0, tiled=True)
    return (loading_grad, factor_grad)


def solution(mesh):
    return jax.shard_map(
        on_device,
        mesh=mesh,
        in_specs=(
            P(None, None, "path"),
            P(None, None, "trade"),
            P("trade"),
            P("trade"),
            P(),
            P(),
            P("trade"),
            P("trade"),
            P("trade"),
        ),
        out_specs=(P("path", None, "trade"), P("trade", None, "path")),
        check_vma=False,
    )
```

profile of v0, /device:TPU:0, one launch (start us, length us, event | category | flops | bytes accessed | tf_op | source)
XLA Modules:
  0.0 284.7 jit_solution(14998099556894631179)
XLA Ops:
  7.2 6.5 %all-to-all-start = ((bf16[32,8,128]{2,1,0:T(8,128)(2,1)}), bf16[32,8,128]{2,1,0:T(8,128)(2,1)S(1)}, u32[]{:S(2)}, u32[]{:S(2)}) async-start(bf16[32,8,128]{2,1,0:T(8,128)(2,1)} %param.13), calls=%async_computation | async-start | bytes 131072 | tf_op jit(solution)/shard_map/all_to_all | solution.py:29
  14.5 4.9 %all-to-all-done = bf16[32,8,128]{2,1,0:T(8,128)(2,1)S(1)} async-done(((bf16[32,8,128]{2,1,0:T(8,128)(2,1)}), bf16[32,8,128]{2,1,0:T(8,128)(2,1)S(1)}, u32[]{:S(2)}, u32[]{:S(2)}) %all-to-all-start) | async-done | bytes 65568 | tf_op jit(solution)/shard_map/all_to_all | solution.py:29
  19.5 50.6 %while.26 = (s32[]{:T(128)}, f32[8,1,512,128]{3,2,1,0:T(8,128)}, bf16[8,1,512,128]{3,2,1,0:T(8,128)(2,1)}, f32[4096]{0:T(1024)}, bf16[8,1,8,512]{3,2,1,0:T(8,128...) while((s32[]{:T(128)}, f32[8,1,512,128]{3,2,1,0:T(8,128)}, ...), condition=%wide.region_1.2_spmd.clone, body=%wide.region_0.1_spmd.clone.sunk | while | flops 1216774272 | bytes 1573053 | solution.py:74
  19.5 3.3 %fusion.88 = f32[1,512,256]{2,1,0:T(8,128)S(1)} fusion(s32[4096]{0:T(1024)} %get-tuple-element.392, f32[4096]{0:T(1024)} %get-tuple-element.389, f32[4096]{0:T(1024)} %get-tuple-element.386, bf16[8,1,8,4096]{3,2,1,0:T(8,128)(2,1)S(1)} %get-tuple-element.388, s32[]{:T(128)} %get-tuple-element.371, bf16[8,1,8,512]{3,2,1,0:T(8,128)(2,1)S(1)} %get-tuple-element.387), kind=kOutput, calls=%fused_computation.9.clone.1 | convolution fusion | flops 1115684864 | bytes 648192 | tf_op jit(solution)/shard_map/while/body/eval_jaxpr/bpk,ks->bps/dot_general | solution.py:57
  25.8 3.3 %fusion.88 = f32[1,512,256]{2,1,0:T(8,128)S(1)} fusion(s32[4096]{0:T(1024)} %get-tuple-element.392, f32[4096]{0:T(1024)} %get-tuple-element.389, f32[4096]{0:T(1024)} %get-tuple-element.386, bf16[8,1,8,4096]{3,2,1,0:T(8,128)(2,1)S(1)} %get-tuple-element.388, s32[]{:T(128)} %get-tuple-element.371, bf16[8,1,8,512]{3,2,1,0:T(8,128)(2,1)S(1)} %get-tuple-element.387), kind=kOutput, calls=%fused_computation.9.clone.1 | convolution fusion | flops 1115684864 | bytes 648192 | tf_op jit(solution)/shard_map/while/body/eval_jaxpr/bpk,ks->bps/dot_general | solution.py:57
  32.1 3.3 %fusion.88 = f32[1,512,256]{2,1,0:T(8,128)S(1)} fusion(s32[4096]{0:T(1024)} %get-tuple-element.392, f32[4096]{0:T(1024)} %get-tuple-element.389, f32[4096]{0:T(1024)} %get-tuple-element.386, bf16[8,1,8,4096]{3,2,1,0:T(8,128)(2,1)S(1)} %get-tuple-element.388, s32[]{:T(128)} %get-tuple-element.371, bf16[8,1,8,512]{3,2,1,0:T(8,128)(2,1)S(1)} %get-tuple-element.387), kind=kOutput, calls=%fused_computation.9.clone.1 | convolution fusion | flops 1115684864 | bytes 648192 | tf_op jit(solution)/shard_map/while/body/eval_jaxpr/bpk,ks->bps/dot_general | solution.py:57
  38.4 3.3 %fusion.88 = f32[1,512,256]{2,1,0:T(8,128)S(1)} fusion(s32[4096]{0:T(1024)} %get-tuple-element.392, f32[4096]{0:T(1024)} %get-tuple-element.389, f32[4096]{0:T(1024)} %get-tuple-element.386, bf16[8,1,8,4096]{3,2,1,0:T(8,128)(2,1)S(1)} %get-tuple-element.388, s32[]{:T(128)} %get-tuple-element.371, bf16[8,1,8,512]{3,2,1,0:T(8,128)(2,1)S(1)} %get-tuple-element.387), kind=kOutput, calls=%fused_computation.9.clone.1 | convolution fusion | flops 1115684864 | bytes 648192 | tf_op jit(solution)/shard_map/while/body/eval_jaxpr/bpk,ks->bps/dot_general | solution.py:57
  44.7 3.3 %fusion.88 = f32[1,512,256]{2,1,0:T(8,128)S(1)} fusion(s32[4096]{0:T(1024)} %get-tuple-element.392, f32[4096]{0:T(1024)} %get-tuple-element.389, f32[4096]{0:T(1024)} %get-tuple-element.386, bf16[8,1,8,4096]{3,2,1,0:T(8,128)(2,1)S(1)} %get-tuple-element.388, s32[]{:T(128)} %get-tuple-element.371, bf16[8,1,8,512]{3,2,1,0:T(8,128)(2,1)S(1)} %get-tuple-element.387), kind=kOutput, calls=%fused_computation.9.clone.1 | convolution fusion | flops 1115684864 | bytes 648192 | tf_op jit(solution)/shard_map/while/body/eval_jaxpr/bpk,ks->bps/dot_general | solution.py:57
  51.0 3.3 %fusion.88 = f32[1,512,256]{2,1,0:T(8,128)S(1)} fusion(s32[4096]{0:T(1024)} %get-tuple-element.392, f32[4096]{0:T(1024)} %get-tuple-element.389, f32[4096]{0:T(1024)} %get-tuple-element.386, bf16[8,1,8,4096]{3,2,1,0:T(8,128)(2,1)S(1)} %get-tuple-element.388, s32[]{:T(128)} %get-tuple-element.371, bf16[8,1,8,512]{3,2,1,0:T(8,128)(2,1)S(1)} %get-tuple-element.387), kind=kOutput, calls=%fused_computation.9.clone.1 | convolution fusion | flops 1115684864 | bytes 648192 | tf_op jit(solution)/shard_map/while/body/eval_jaxpr/bpk,ks->bps/dot_general | solution.py:57
  57.3 3.3 %fusion.88 = f32[1,512,256]{2,1,0:T(8,128)S(1)} fusion(s32[4096]{0:T(1024)} %get-tuple-element.392, f32[4096]{0:T(1024)} %get-tuple-element.389, f32[4096]{0:T(1024)} %get-tuple-element.386, bf16[8,1,8,4096]{3,2,1,0:T(8,128)(2,1)S(1)} %get-tuple-element.388, s32[]{:T(128)} %get-tuple-element.371, bf16[8,1,8,512]{3,2,1,0:T(8,128)(2,1)S(1)} %get-tuple-element.387), kind=kOutput, calls=%fused_computation.9.clone.1 | convolution fusion | flops 1115684864 | bytes 648192 | tf_op jit(solution)/shard_map/while/body/eval_jaxpr/bpk,ks->bps/dot_general | solution.py:57
  63.7 3.3 %fusion.88 = f32[1,512,256]{2,1,0:T(8,128)S(1)} fusion(s32[4096]{0:T(1024)} %get-tuple-element.392, f32[4096]{0:T(1024)} %get-tuple-element.389, f32[4096]{0:T(1024)} %get-tuple-element.386, bf16[8,1,8,4096]{3,2,1,0:T(8,128)(2,1)S(1)} %get-tuple-element.388, s32[]{:T(128)} %get-tuple-element.371, bf16[8,1,8,512]{3,2,1,0:T(8,128)(2,1)S(1)} %get-tuple-element.387), kind=kOutput, calls=%fused_computation.9.clone.1 | convolution fusion | flops 1115684864 | bytes 648192 | tf_op jit(solution)/shard_map/while/body/eval_jaxpr/bpk,ks->bps/dot_general | solution.py:57
  70.9 59.7 %all-reduce.2.cloned.1.call-done = f32[8,512,128]{2,1,0:T(8,128)} async-done(((f32[8,512,128]{2,1,0:T(8,128)}), f32[8,512,128]{2,1,0:T(8,128)}) %all-reduce.2.cloned.1.call-update) | async-done | bytes 2097168 | tf_op jit(solution)/shard_map/psum | solution.py:76
  132.7 88.6 %while.27 = (s32[]{:T(128)}, f32[8,1,8,4096]{3,2,1,0:T(8,128)}, f32[8,1,8,512]{3,2,1,0:T(8,128)}, bf16[8,1,8,512]{3,2,1,0:T(8,128)(2,1)S(1)}, bf16[8,1,512,128]{...) while((s32[]{:T(128)}, f32[8,1,8,4096]{3,2,1,0:T(8,128)}, ...), condition=%wide.region_4.5_spmd.clone, body=%wide.region_3.4_spmd.clone.sunk | while | flops 1200193536 | bytes 31266512 | solution.py:101
  145.7 2.6 fusion.100
  178.9 2.6 fusion.100
  207.5 2.6 fusion.102
  212.1 2.6 fusion.100
  218.6 2.6 fusion.102
  221.3 2.9 %copy.18 = f32[8,1,8,512]{2,0,3,1:T(8,128)} copy(f32[8,1,8,512]{3,2,1,0:T(8,128)} %get-tuple-element.445) | data formatting | bytes 262144 | tf_op jit(solution)/shard_map/while | solution.py:101
  224.1 3.1 %bitcast_bitcast_fusion = f32[512,8,8]{2,1,0:T(8,128)} fusion(f32[8,1,8,512]{2,0,3,1:T(8,128)} %copy.18), kind=kLoop, calls=%fused_computation.71 | loop fusion | bytes 262144
  227.2 2.7 reshape.144
  229.8 10.2 %all_to_all.33 = f32[4,1,8192]{2,1,0:T(1,128)S(1)} all-to-all(f32[4,1,8192]{2,1,0:T(1,128)S(1)} %reshape.144), channel_id=1, replica_groups=mesh['path'=4,'trade'=8] {'path'}, dimensions={0} | all-to-all | bytes 262144 | tf_op jit(solution)/shard_map/all_to_all | solution.py:107
  244.1 2.8 copy.19
  249.2 28.7 %reduce-scatter.2.cloned.1.call-done = f32[4,8,128]{2,1,0:T(8,128)} async-done(((f32[32,8,128]{2,1,0:T(8,128)}), f32[4,8,128]{2,1,0:T(8,128)}) %reduce-scatter.2.cloned.1.call-update) | async-done | bytes 16400 | tf_op jit(solution)/shard_map/reduce_scatter | solution.py:108
  (193 shorter events, 109.0 us)
Async XLA Ops:
  7.2 6.5 %copy-start = (bf16[32,8,4096]{2,1,0:T(8,128)(2,1)S(1)}, bf16[32,8,4096]{2,1,0:T(8,128)(2,1)}, u32[]{:S(2)}) copy-start(bf16[32,8,4096]{2,1,0:T(8,128)(2,1)} %param.14) | copy-start | bytes 6291460
  7.2 12.2 %all-to-all-start = ((bf16[32,8,128]{2,1,0:T(8,128)(2,1)}), bf16[32,8,128]{2,1,0:T(8,128)(2,1)S(1)}, u32[]{:S(2)}, u32[]{:S(2)}) async-start(bf16[32,8,128]{2,1,0:T(8,128)(2,1)} %param.13), calls=%async_computation | async-start | bytes 131072 | tf_op jit(solution)/shard_map/all_to_all | solution.py:29
  13.7 116.8 %all-reduce.2.cloned.1.call-start = ((), (), s32[]{:S(2)}) async-start(), calls=%async_computation.3 | async-start | bytes 4194304 | tf_op jit(solution)/shard_map/psum | solution.py:76
  19.4 50.7 %copy-start.10 = (f32[32]{0:T(128)S(1)}, f32[32]{0:T(128)}, u32[]{:S(2)}) copy-start(f32[32]{0:T(128)} %param.17) | copy-start | bytes 388
  19.4 50.7 %copy-start.8 = (f32[128]{0:T(128)S(1)}, f32[128]{0:T(128)}, u32[]{:S(2)}) copy-start(f32[128]{0:T(128)} %param.18) | copy-start | bytes 1540
  19.5 5.2 %copy-start.5 = (s32[128]{0:T(128)S(1)}, s32[128]{0:T(128)}, u32[]{:S(2)}) copy-start(s32[128]{0:T(128)} %get-tuple-element.393) | copy-start | bytes 1540 | tf_op jit(solution)/shard_map/while
  25.8 5.2 %copy-start.5 = (s32[128]{0:T(128)S(1)}, s32[128]{0:T(128)}, u32[]{:S(2)}) copy-start(s32[128]{0:T(128)} %get-tuple-element.393) | copy-start | bytes 1540 | tf_op jit(solution)/shard_map/while
  32.1 5.2 %copy-start.5 = (s32[128]{0:T(128)S(1)}, s32[128]{0:T(128)}, u32[]{:S(2)}) copy-start(s32[128]{0:T(128)} %get-tuple-element.393) | copy-start | bytes 1540 | tf_op jit(solution)/shard_map/while
  38.4 5.1 %copy-start.5 = (s32[128]{0:T(128)S(1)}, s32[128]{0:T(128)}, u32[]{:S(2)}) copy-start(s32[128]{0:T(128)} %get-tuple-element.393) | copy-start | bytes 1540 | tf_op jit(solution)/shard_map/while
  44.7 5.2 %copy-start.5 = (s32[128]{0:T(128)S(1)}, s32[128]{0:T(128)}, u32[]{:S(2)}) copy-start(s32[128]{0:T(128)} %get-tuple-element.393) | copy-start | bytes 1540 | tf_op jit(solution)/shard_map/while
  51.0 5.2 %copy-start.5 = (s32[128]{0:T(128)S(1)}, s32[128]{0:T(128)}, u32[]{:S(2)}) copy-start(s32[128]{0:T(128)} %get-tuple-element.393) | copy-start | bytes 1540 | tf_op jit(solution)/shard_map/while
  57.3 5.2 %copy-start.5 = (s32[128]{0:T(128)S(1)}, s32[128]{0:T(128)}, u32[]{:S(2)}) copy-start(s32[128]{0:T(128)} %get-tuple-element.393) | copy-start | bytes 1540 | tf_op jit(solution)/shard_map/while
  63.7 5.2 %copy-start.5 = (s32[128]{0:T(128)S(1)}, s32[128]{0:T(128)}, u32[]{:S(2)}) copy-start(s32[128]{0:T(128)} %get-tuple-element.393) | copy-start | bytes 1540 | tf_op jit(solution)/shard_map/while
  70.0 62.6 %copy-start.2 = (f32[4096]{0:T(1024)S(1)}, f32[4096]{0:T(1024)}, u32[]{:S(2)}) copy-start(f32[4096]{0:T(1024)} %get-tuple-element.436) | copy-start | bytes 49156
  70.0 62.7 %copy-start.6 = (s32[128]{0:T(128)S(1)}, s32[128]{0:T(128)}, u32[]{:S(2)}) copy-start(s32[128]{0:T(128)} %get-tuple-element.442) | copy-start | bytes 1540
  70.0 207.8 %reduce-scatter.2.cloned.1.call-start = ((), (), s32[]{:S(2)}) async-start(), calls=%async_computation.4 | async-start | bytes 147456 | tf_op jit(solution)/shard_map/reduce_scatter | solution.py:108
  139.8 4.0 %copy-start.7 = (s32[128]{0:T(128)S(1)}, s32[128]{0:T(128)}, u32[]{:S(2)}) copy-start(s32[128]{0:T(128)} %get-tuple-element.454) | copy-start | bytes 1540 | tf_op jit(solution)/shard_map/while
  150.9 4.0 %copy-start.7 = (s32[128]{0:T(128)S(1)}, s32[128]{0:T(128)}, u32[]{:S(2)}) copy-start(s32[128]{0:T(128)} %get-tuple-element.454) | copy-start | bytes 1540 | tf_op jit(solution)/shard_map/while
  161.9 4.0 %copy-start.7 = (s32[128]{0:T(128)S(1)}, s32[128]{0:T(128)}, u32[]{:S(2)}) copy-start(s32[128]{0:T(128)} %get-tuple-element.454) | copy-start | bytes 1540 | tf_op jit(solution)/shard_map/while
  173.0 4.0 %copy-start.7 = (s32[128]{0:T(128)S(1)}, s32[128]{0:T(128)}, u32[]{:S(2)}) copy-start(s32[128]{0:T(128)} %get-tuple-element.454) | copy-start | bytes 1540 | tf_op jit(solution)/shard_map/while
  184.1 4.0 %copy-start.7 = (s32[128]{0:T(128)S(1)}, s32[128]{0:T(128)}, u32[]{:S(2)}) copy-start(s32[128]{0:T(128)} %get-tuple-element.454) | copy-start | bytes 1540 | tf_op jit(solution)/shard_map/while
  195.1 4.0 %copy-start.7 = (s32[128]{0:T(128)S(1)}, s32[128]{0:T(128)}, u32[]{:S(2)}) copy-start(s32[128]{0:T(128)} %get-tuple-element.454) | copy-start | bytes 1540 | tf_op jit(solution)/shard_map/while
  206.2 4.0 %copy-start.7 = (s32[128]{0:T(128)S(1)}, s32[128]{0:T(128)}, u32[]{:S(2)}) copy-start(s32[128]{0:T(128)} %get-tuple-element.454) | copy-start | bytes 1540 | tf_op jit(solution)/shard_map/while
  217.3 4.0 %copy-start.7 = (s32[128]{0:T(128)S(1)}, s32[128]{0:T(128)}, u32[]{:S(2)}) copy-start(s32[128]{0:T(128)} %get-tuple-element.454) | copy-start | bytes 1540 | tf_op jit(solution)/shard_map/while
  (25 other events, 57.3 us)
Sparse Core Ops, SparseCore 0:
  70.2 60.2 all-reduce.1
  247.0 30.8 reduce-scatter.1
where the time goes:
time: 287 us; the launch traced here: 285 us
  matrix products  110 us (38%)
  waiting for transfers between devices  93.3 us (33%)
  local copies, waits for them, and re-layouts  33.8 us (12%)
  other arithmetic  15.8 us (6%)
  between operations  14.1 us (5%)
  blocking collectives  10.2 us (4%)
  starting transfers between devices  6.53 us (2%)
    psum x1, waiting for transfers between devices, on_device(): span_total = lax.psum(span_parts, 'trade')  59.7 us
    reduce_scatter x1, waiting for transfers between devices, on_device(): lax.psum_scatter(regrouped, 'trade', scatter_dimension=0, tiled=True)  28.7 us
    dot_general x8, matrix products, forward(): jnp.einsum('bpk,ks->bps', values, slot_table, preferred_element_type=jnp....  26.4 us
    dot_general x8, matrix products, adjoint(): jnp.einsum('bps,ks->bpk', slot_weight, slot_table, preferred_element_type...  21.1 us
    dot_general x8, matrix products, adjoint(): jnp.einsum('bfk,bpk->bfp', loading_block, sensitivity, preferred_element_...  21.1 us
    dot_general x8, matrix products, price(): jnp.einsum('bfp,bfk->bpk', factor_block, loading_block, preferred_element...  20.3 us
    dot_general x8, matrix products, adjoint(): jnp.einsum('bfp,bpk->bfk', factor_block, sensitivity, preferred_element_t...  10.5 us
    all_to_all x1, blocking collectives, on_device(): lax.all_to_all(factor_terms, 'path', split_axis=2, concat_axis=0, tiled=T...  10.2 us
  transfers between devices with their start and end apart: 3, of which 3 were waited for; matrix products, arithmetic and copies ran while one was open for 1% of the time, Pallas kernels for 0%

commit v1 on v0

--- a/solution.py
+++ b/solution.py
@@ -73,7 +73,11 @@
 
     span_parts, local_weights = lax.map(forward, (factor_blocks, loading_blocks, weight_blocks))
     span_parts = span_parts.reshape(date_count, path_local, span_count)
-    span_total = lax.psum(span_parts, "trade")
+    span_total = span_parts
+    for hop in (1, 2, 4):
+        span_total = span_total + lax.ppermute(
+            span_total, "trade", [(dev, dev ^ hop) for dev in range(8)]
+        )
     span_weight = (
         weight_here[:, None, None] * loss_spanning * jax.nn.sigmoid(span_total / smoothing)
     ).astype(jnp.bfloat16)

time: 287 us -> 330 us (1.15)
  waiting for transfers between devices: 93.3 us -> 131 us
  other arithmetic: 15.8 us -> 19.9 us
    ppermute x0 -> x3, waiting for transfers between devices: none -> 96 us  [on_device(): lax.ppermute(span_total, 'trade', [(dev, dev ^ hop) for dev in range(8)])]
    psum x1 -> x0, waiting for transfers between devices: 59.7 us -> none  [on_device(): span_total = lax.psum(span_parts, 'trade')]
    add x0 -> x2, other arithmetic: none -> 3.4 us  [on_device(): span_total + lax.ppermute(span_total, 'trade', [(dev, dev ^ hop) for dev...]
  transfers between devices with their start and end apart: 3 -> 5, of which waited for: 3 -> 5; matrix products, arithmetic and copies ran while one was open for 1% -> 1% of each run, Pallas kernels for 0% -> 0%
where the time goes in v1:
time: 330 us; the launch traced here: 328 us
  waiting for transfers between devices  131 us (40%)
  matrix products  110 us (33%)
  local copies, waits for them, and re-layouts  33.3 us (10%)
  other arithmetic  19.9 us (6%)
  between operations  14.1 us (4%)
  starting transfers between devices  9.57 us (3%)
  blocking collectives  8.31 us (3%)
    ppermute x3, waiting for transfers between devices, on_device(): lax.ppermute(span_total, 'trade', [(dev, dev ^ hop) for dev in range(8)])  96 us
    reduce_scatter x1, waiting for transfers between devices, on_device(): lax.psum_scatter(regrouped, 'trade', scatter_dimension=0, tiled=True)  30.5 us
    dot_general x8, matrix products, forward(): jnp.einsum('bpk,ks->bps', values, slot_table, preferred_element_type=jnp....  26.4 us
    dot_general x8, matrix products, adjoint(): jnp.einsum('bfk,bpk->bfp', loading_block, sensitivity, preferred_element_...  21.2 us
    dot_general x8, matrix products, adjoint(): jnp.einsum('bps,ks->bpk', slot_weight, slot_table, preferred_element_type...  21.1 us
    dot_general x8, matrix products, price(): jnp.einsum('bfp,bfk->bpk', factor_block, loading_block, preferred_element...  20.3 us
    dot_general x8, matrix products, adjoint(): jnp.einsum('bfp,bpk->bfk', factor_block, sensitivity, preferred_element_t...  10.5 us
    dot_general x8, matrix products, forward(): jnp.einsum('bps,sn->bpn', partial_sums[:, :, :span_local], set_table, pre...  9.17 us
  transfers between devices with their start and end apart: 5, of which 5 were waited for; matrix products, arithmetic and copies ran while one was open for 1% of the time, Pallas kernels for 0%

profile of v1, /device:TPU:0, one launch (start us, length us, event | category | flops | bytes accessed | tf_op | source)
XLA Modules:
  0.0 327.5 jit_solution(11563548764530204331)
XLA Ops:
  7.2 6.5 %all-to-all-start = ((bf16[32,8,128]{2,1,0:T(8,128)(2,1)}), bf16[32,8,128]{2,1,0:T(8,128)(2,1)S(1)}, u32[]{:S(2)}, u32[]{:S(2)}) async-start(bf16[32,8,128]{2,1,0:T(8,128)(2,1)} %param.13), calls=%async_computation | async-start | bytes 131072 | tf_op jit(solution)/shard_map/all_to_all | solution.py:29
  14.5 4.9 %all-to-all-done = bf16[32,8,128]{2,1,0:T(8,128)(2,1)S(1)} async-done(((bf16[32,8,128]{2,1,0:T(8,128)(2,1)}), bf16[32,8,128]{2,1,0:T(8,128)(2,1)S(1)}, u32[]{:S(2)}, u32[]{:S(2)}) %all-to-all-start) | async-done | bytes 65568 | tf_op jit(solution)/shard_map/all_to_all | solution.py:29
  19.4 50.8 %while.26 = (s32[]{:T(128)}, f32[8,1,512,128]{3,2,1,0:T(8,128)}, bf16[8,1,512,128]{3,2,1,0:T(8,128)(2,1)}, f32[4096]{0:T(1024)}, bf16[8,1,8,512]{3,2,1,0:T(8,128...) while((s32[]{:T(128)}, f32[8,1,512,128]{3,2,1,0:T(8,128)}, ...), condition=%wide.region_1.2_spmd.clone, body=%wide.region_0.1_spmd.clone.sunk | while | flops 1216774272 | bytes 1573053 | solution.py:74
  19.5 3.3 %fusion.88 = f32[1,512,256]{2,1,0:T(8,128)S(1)} fusion(s32[4096]{0:T(1024)} %get-tuple-element.392, f32[4096]{0:T(1024)} %get-tuple-element.389, f32[4096]{0:T(1024)} %get-tuple-element.386, bf16[8,1,8,4096]{3,2,1,0:T(8,128)(2,1)S(1)} %get-tuple-element.388, s32[]{:T(128)} %get-tuple-element.371, bf16[8,1,8,512]{3,2,1,0:T(8,128)(2,1)S(1)} %get-tuple-element.387), kind=kOutput, calls=%fused_computation.9.clone.1 | convolution fusion | flops 1115684864 | bytes 648192 | tf_op jit(solution)/shard_map/while/body/eval_jaxpr/bpk,ks->bps/dot_general | solution.py:57
  25.8 3.3 %fusion.88 = f32[1,512,256]{2,1,0:T(8,128)S(1)} fusion(s32[4096]{0:T(1024)} %get-tuple-element.392, f32[4096]{0:T(1024)} %get-tuple-element.389, f32[4096]{0:T(1024)} %get-tuple-element.386, bf16[8,1,8,4096]{3,2,1,0:T(8,128)(2,1)S(1)} %get-tuple-element.388, s32[]{:T(128)} %get-tuple-element.371, bf16[8,1,8,512]{3,2,1,0:T(8,128)(2,1)S(1)} %get-tuple-element.387), kind=kOutput, calls=%fused_computation.9.clone.1 | convolution fusion | flops 1115684864 | bytes 648192 | tf_op jit(solution)/shard_map/while/body/eval_jaxpr/bpk,ks->bps/dot_general | solution.py:57
  32.1 3.3 %fusion.88 = f32[1,512,256]{2,1,0:T(8,128)S(1)} fusion(s32[4096]{0:T(1024)} %get-tuple-element.392, f32[4096]{0:T(1024)} %get-tuple-element.389, f32[4096]{0:T(1024)} %get-tuple-element.386, bf16[8,1,8,4096]{3,2,1,0:T(8,128)(2,1)S(1)} %get-tuple-element.388, s32[]{:T(128)} %get-tuple-element.371, bf16[8,1,8,512]{3,2,1,0:T(8,128)(2,1)S(1)} %get-tuple-element.387), kind=kOutput, calls=%fused_computation.9.clone.1 | convolution fusion | flops 1115684864 | bytes 648192 | tf_op jit(solution)/shard_map/while/body/eval_jaxpr/bpk,ks->bps/dot_general | solution.py:57
  38.5 3.3 %fusion.88 = f32[1,512,256]{2,1,0:T(8,128)S(1)} fusion(s32[4096]{0:T(1024)} %get-tuple-element.392, f32[4096]{0:T(1024)} %get-tuple-element.389, f32[4096]{0:T(1024)} %get-tuple-element.386, bf16[8,1,8,4096]{3,2,1,0:T(8,128)(2,1)S(1)} %get-tuple-element.388, s32[]{:T(128)} %get-tuple-element.371, bf16[8,1,8,512]{3,2,1,0:T(8,128)(2,1)S(1)} %get-tuple-element.387), kind=kOutput, calls=%fused_computation.9.clone.1 | convolution fusion | flops 1115684864 | bytes 648192 | tf_op jit(solution)/shard_map/while/body/eval_jaxpr/bpk,ks->bps/dot_general | solution.py:57
  44.8 3.3 %fusion.88 = f32[1,512,256]{2,1,0:T(8,128)S(1)} fusion(s32[4096]{0:T(1024)} %get-tuple-element.392, f32[4096]{0:T(1024)} %get-tuple-element.389, f32[4096]{0:T(1024)} %get-tuple-element.386, bf16[8,1,8,4096]{3,2,1,0:T(8,128)(2,1)S(1)} %get-tuple-element.388, s32[]{:T(128)} %get-tuple-element.371, bf16[8,1,8,512]{3,2,1,0:T(8,128)(2,1)S(1)} %get-tuple-element.387), kind=kOutput, calls=%fused_computation.9.clone.1 | convolution fusion | flops 1115684864 | bytes 648192 | tf_op jit(solution)/shard_map/while/body/eval_jaxpr/bpk,ks->bps/dot_general | solution.py:57
  51.2 3.3 %fusion.88 = f32[1,512,256]{2,1,0:T(8,128)S(1)} fusion(s32[4096]{0:T(1024)} %get-tuple-element.392, f32[4096]{0:T(1024)} %get-tuple-element.389, f32[4096]{0:T(1024)} %get-tuple-element.386, bf16[8,1,8,4096]{3,2,1,0:T(8,128)(2,1)S(1)} %get-tuple-element.388, s32[]{:T(128)} %get-tuple-element.371, bf16[8,1,8,512]{3,2,1,0:T(8,128)(2,1)S(1)} %get-tuple-element.387), kind=kOutput, calls=%fused_computation.9.clone.1 | convolution fusion | flops 1115684864 | bytes 648192 | tf_op jit(solution)/shard_map/while/body/eval_jaxpr/bpk,ks->bps/dot_general | solution.py:57
  57.5 3.3 %fusion.88 = f32[1,512,256]{2,1,0:T(8,128)S(1)} fusion(s32[4096]{0:T(1024)} %get-tuple-element.392, f32[4096]{0:T(1024)} %get-tuple-element.389, f32[4096]{0:T(1024)} %get-tuple-element.386, bf16[8,1,8,4096]{3,2,1,0:T(8,128)(2,1)S(1)} %get-tuple-element.388, s32[]{:T(128)} %get-tuple-element.371, bf16[8,1,8,512]{3,2,1,0:T(8,128)(2,1)S(1)} %get-tuple-element.387), kind=kOutput, calls=%fused_computation.9.clone.1 | convolution fusion | flops 1115684864 | bytes 648192 | tf_op jit(solution)/shard_map/while/body/eval_jaxpr/bpk,ks->bps/dot_general | solution.py:57
  63.8 3.3 %fusion.88 = f32[1,512,256]{2,1,0:T(8,128)S(1)} fusion(s32[4096]{0:T(1024)} %get-tuple-element.392, f32[4096]{0:T(1024)} %get-tuple-element.389, f32[4096]{0:T(1024)} %get-tuple-element.386, bf16[8,1,8,4096]{3,2,1,0:T(8,128)(2,1)S(1)} %get-tuple-element.388, s32[]{:T(128)} %get-tuple-element.371, bf16[8,1,8,512]{3,2,1,0:T(8,128)(2,1)S(1)} %get-tuple-element.387), kind=kOutput, calls=%fused_computation.9.clone.1 | convolution fusion | flops 1115684864 | bytes 648192 | tf_op jit(solution)/shard_map/while/body/eval_jaxpr/bpk,ks->bps/dot_general | solution.py:57
  70.2 4.4 %collective-permute-done = f32[8,512,128]{2,1,0:T(8,128)S(1)} collective-permute-done((f32[8,512,128]{2,1,0:T(8,128)}, f32[8,512,128]{2,1,0:T(8,128)S(1)}, u32[]{:S(2)}, u32[]{:S(2)}) %collective-permute-start) | collective-permute-done | bytes 2097184 | tf_op jit(solution)/shard_map/ppermute | solution.py:78
  78.0 46.2 %collective-permute-done.1 = f32[8,512,128]{2,1,0:T(8,128)S(1)} collective-permute-done((f32[8,512,128]{2,1,0:T(8,128)S(1)}, f32[8,512,128]{2,1,0:T(8,128)S(1)}, u32[]{:S(2)}, u32[]{:S(2)}) %collective-permute-start.1) | collective-permute-done | bytes 2097184 | tf_op jit(solution)/shard_map/ppermute | solution.py:78
  127.4 45.5 %collective-permute-done.2 = f32[8,512,128]{2,1,0:T(8,128)} collective-permute-done((f32[8,512,128]{2,1,0:T(8,128)}, f32[8,512,128]{2,1,0:T(8,128)}, u32[]{:S(2)}, u32[]{:S(2)}) %collective-permute-start.2) | collective-permute-done | bytes 2097184 | tf_op jit(solution)/shard_map/ppermute | solution.py:78
  172.9 2.8 fusion.62
  175.7 88.5 %while.27 = (s32[]{:T(128)}, f32[8,1,8,4096]{3,2,1,0:T(8,128)}, f32[8,1,8,512]{3,2,1,0:T(8,128)}, bf16[8,1,8,512]{3,2,1,0:T(8,128)(2,1)S(1)}, bf16[8,1,512,128]{...) while((s32[]{:T(128)}, f32[8,1,8,4096]{3,2,1,0:T(8,128)}, ...), condition=%wide.region_3.4_spmd.clone, body=%wide.region_2.3_spmd.clone.sunk | while | flops 1200193536 | bytes 31266512 | solution.py:105
  217.3 2.7 fusion.102
  228.4 2.6 fusion.102
  264.2 2.9 copy.18
  267.0 3.1 bitcast_bitcast_fusion
  270.1 2.7 reshape.144
  272.8 8.3 %all_to_all.33 = f32[4,1,8192]{2,1,0:T(1,128)S(1)} all-to-all(f32[4,1,8192]{2,1,0:T(1,128)S(1)} %reshape.144), channel_id=1, replica_groups=mesh['path'=4,'trade'=8] {'path'}, dimensions={0} | all-to-all | bytes 262144 | tf_op jit(solution)/shard_map/all_to_all | solution.py:111
  285.1 2.8 copy.19
  290.2 30.5 %reduce-scatter.2.cloned.1.call-done = f32[4,8,128]{2,1,0:T(8,128)} async-done(((f32[32,8,128]{2,1,0:T(8,128)}), f32[4,8,128]{2,1,0:T(8,128)}) %reduce-scatter.2.cloned.1.call-update) | async-done | bytes 16400 | tf_op jit(solution)/shard_map/reduce_scatter | solution.py:112
  (198 shorter events, 120.8 us)
Async XLA Ops:
  7.2 6.5 %copy-start = (bf16[32,8,4096]{2,1,0:T(8,128)(2,1)S(1)}, bf16[32,8,4096]{2,1,0:T(8,128)(2,1)}, u32[]{:S(2)}) copy-start(bf16[32,8,4096]{2,1,0:T(8,128)(2,1)} %param.14) | copy-start | bytes 6291460
  7.2 12.2 %all-to-all-start = ((bf16[32,8,128]{2,1,0:T(8,128)(2,1)}), bf16[32,8,128]{2,1,0:T(8,128)(2,1)S(1)}, u32[]{:S(2)}, u32[]{:S(2)}) async-start(bf16[32,8,128]{2,1,0:T(8,128)(2,1)} %param.13), calls=%async_computation | async-start | bytes 131072 | tf_op jit(solution)/shard_map/all_to_all | solution.py:29
  13.7 307.0 %reduce-scatter.2.cloned.1.call-start = ((), (), s32[]{:S(2)}) async-start(), calls=%async_computation.3 | async-start | bytes 147456 | tf_op jit(solution)/shard_map/reduce_scatter | solution.py:112
  19.4 3.9 %copy-start.9 = (f32[128]{0:T(128)S(1)}, f32[128]{0:T(128)}, u32[]{:S(2)}) copy-start(f32[128]{0:T(128)} %get-tuple-element.391) | copy-start | bytes 1540 | tf_op jit(solution)/shard_map/while
  19.5 5.2 %copy-start.5 = (s32[128]{0:T(128)S(1)}, s32[128]{0:T(128)}, u32[]{:S(2)}) copy-start(s32[128]{0:T(128)} %get-tuple-element.393) | copy-start | bytes 1540 | tf_op jit(solution)/shard_map/while
  25.8 5.2 %copy-start.5 = (s32[128]{0:T(128)S(1)}, s32[128]{0:T(128)}, u32[]{:S(2)}) copy-start(s32[128]{0:T(128)} %get-tuple-element.393) | copy-start | bytes 1540 | tf_op jit(solution)/shard_map/while
  32.1 3.9 %copy-start.9 = (f32[128]{0:T(128)S(1)}, f32[128]{0:T(128)}, u32[]{:S(2)}) copy-start(f32[128]{0:T(128)} %get-tuple-element.391) | copy-start | bytes 1540 | tf_op jit(solution)/shard_map/while
  32.1 5.2 %copy-start.5 = (s32[128]{0:T(128)S(1)}, s32[128]{0:T(128)}, u32[]{:S(2)}) copy-start(s32[128]{0:T(128)} %get-tuple-element.393) | copy-start | bytes 1540 | tf_op jit(solution)/shard_map/while
  38.5 3.9 %copy-start.9 = (f32[128]{0:T(128)S(1)}, f32[128]{0:T(128)}, u32[]{:S(2)}) copy-start(f32[128]{0:T(128)} %get-tuple-element.391) | copy-start | bytes 1540 | tf_op jit(solution)/shard_map/while
  38.5 5.2 %copy-start.5 = (s32[128]{0:T(128)S(1)}, s32[128]{0:T(128)}, u32[]{:S(2)}) copy-start(s32[128]{0:T(128)} %get-tuple-element.393) | copy-start | bytes 1540 | tf_op jit(solution)/shard_map/while
  44.8 5.2 %copy-start.5 = (s32[128]{0:T(128)S(1)}, s32[128]{0:T(128)}, u32[]{:S(2)}) copy-start(s32[128]{0:T(128)} %get-tuple-element.393) | copy-start | bytes 1540 | tf_op jit(solution)/shard_map/while
  51.2 5.2 %copy-start.5 = (s32[128]{0:T(128)S(1)}, s32[128]{0:T(128)}, u32[]{:S(2)}) copy-start(s32[128]{0:T(128)} %get-tuple-element.393) | copy-start | bytes 1540 | tf_op jit(solution)/shard_map/while
  57.5 3.9 %copy-start.9 = (f32[128]{0:T(128)S(1)}, f32[128]{0:T(128)}, u32[]{:S(2)}) copy-start(f32[128]{0:T(128)} %get-tuple-element.391) | copy-start | bytes 1540 | tf_op jit(solution)/shard_map/while
  57.5 5.2 %copy-start.5 = (s32[128]{0:T(128)S(1)}, s32[128]{0:T(128)}, u32[]{:S(2)}) copy-start(s32[128]{0:T(128)} %get-tuple-element.393) | copy-start | bytes 1540 | tf_op jit(solution)/shard_map/while
  63.8 3.9 %copy-start.9 = (f32[128]{0:T(128)S(1)}, f32[128]{0:T(128)}, u32[]{:S(2)}) copy-start(f32[128]{0:T(128)} %get-tuple-element.391) | copy-start | bytes 1540 | tf_op jit(solution)/shard_map/while
  63.8 5.2 %copy-start.5 = (s32[128]{0:T(128)S(1)}, s32[128]{0:T(128)}, u32[]{:S(2)}) copy-start(s32[128]{0:T(128)} %get-tuple-element.393) | copy-start | bytes 1540 | tf_op jit(solution)/shard_map/while
  70.2 6.2 %copy-start.1 = (bf16[8,1,8,4096]{3,2,1,0:T(8,128)(2,1)}, bf16[8,1,8,4096]{3,2,1,0:T(8,128)(2,1)S(1)}, u32[]{:S(2)}) copy-start(bf16[8,1,8,4096]{3,2,1,0:T(8,128)(2,1)S(1)} %get-tuple-element.430) | copy-start | bytes 1572868
  70.2 4.4 %collective-permute-start = (f32[8,512,128]{2,1,0:T(8,128)}, f32[8,512,128]{2,1,0:T(8,128)S(1)}, u32[]{:S(2)}, u32[]{:S(2)}) collective-permute-start(f32[8,512,128]{2,1,0:T(8,128)} %bitcast.118), channel_id=1, source_target_pairs={{0,1},{1,0},{2,3},{3,2},{4,5},{5,4},{6,7},{7,6},{8,9},{9,8},{10,11... | collective-permute-start | bytes 6291464 | tf_op jit(solution)/shard_map/ppermute | solution.py:78
  76.4 50.8 %copy-start.10 = (f32[32]{0:T(128)S(1)}, f32[32]{0:T(128)}, u32[]{:S(2)}) copy-start(f32[32]{0:T(128)} %param.17) | copy-start | bytes 388
  76.5 50.9 %copy-start.8 = (f32[128]{0:T(128)S(1)}, f32[128]{0:T(128)}, u32[]{:S(2)}) copy-start(f32[128]{0:T(128)} %param.18) | copy-start | bytes 1540
  76.5 47.7 %collective-permute-start.1 = (f32[8,512,128]{2,1,0:T(8,128)S(1)}, f32[8,512,128]{2,1,0:T(8,128)S(1)}, u32[]{:S(2)}, u32[]{:S(2)}) collective-permute-start(f32[8,512,128]{2,1,0:T(8,128)S(1)} %bitcast_add_fusion), channel_id=1, source_target_pairs={{0,2},{1,3},{2,0},{3,1},{4,6},{5,7},{6,4},{7,5},{8,10},{9,11},{10,... | collective-permute-start | bytes 6291464 | tf_op jit(solution)/shard_map/ppermute | solution.py:78
  125.8 47.1 %collective-permute-start.2 = (f32[8,512,128]{2,1,0:T(8,128)}, f32[8,512,128]{2,1,0:T(8,128)}, u32[]{:S(2)}, u32[]{:S(2)}) collective-permute-start(f32[8,512,128]{2,1,0:T(8,128)} %add.29), channel_id=1, source_target_pairs={{0,4},{1,5},{2,6},{3,7},{4,0},{5,1},{6,2},{7,3},{8,12},{9,13},{10,... | collective-permute-start | bytes 6291464 | tf_op jit(solution)/shard_map/ppermute | solution.py:78
  127.4 48.2 %copy-start.2 = (f32[4096]{0:T(1024)S(1)}, f32[4096]{0:T(1024)}, u32[]{:S(2)}) copy-start(f32[4096]{0:T(1024)} %get-tuple-element.436) | copy-start | bytes 49156
  127.4 48.3 %copy-start.6 = (s32[128]{0:T(128)S(1)}, s32[128]{0:T(128)}, u32[]{:S(2)}) copy-start(s32[128]{0:T(128)} %get-tuple-element.442) | copy-start | bytes 1540
  (27 other events, 58.3 us)
Sparse Core Ops, SparseCore 0:
  288.0 32.6 reduce-scatter.1
